TPU v7x, 128 devices: a whole 4x4x4 slice. The times are simulated.
128 devices in a mesh: sx: 8 (over y, core), sy: 16 (over z, x).
Axes of the slice: x: 4, y: 4, z: 4, core: 2. Of those that a mesh axis runs over, the one named last changes fastest.
Arguments:
- features: bfloat16 [131072, 384], P(('sx', 'sy'))
- cotangent: bfloat16 [131072, 384], P(('sx', 'sy')), may hold values from -6 to 6
- hilbert_rank: int32 [131072], P(('sx', 'sy')), may hold values from 0 to 131071, as said below
- w_qkv: bfloat16 [384, 1152], replicated
- w_proj: bfloat16 [384, 384], replicated, may hold values from -0.3125 to 0.3125
Outputs:
- outputs: bfloat16 [131072, 384], P(('sx', 'sy'))
- grad_features: bfloat16 [131072, 384], P(('sx', 'sy'))
- grad_qkv: float32 [384, 1152], replicated
- grad_proj: float32 [384, 384], replicated
Inputs may be any that keep to these rules, and one draw needn't show every extreme that they name: hilbert_rank is a permutation. Hilbert positions t * 1024 to (t + 1) * 1024 - 1 belong to device t. Every device sends rows to every device, 4 to 16 rows to each, and every device has 16 rows for some owners and receives 16 rows from some devices.
All inputs are finite; a program needn't handle non-finite values.
Results may differ from a plain program's by a relative error of at most 0.004.
The roundings to bfloat16 on the way count: a program that leaves them out, or rounds other values in their place, can miss the bound.
Values may be sent and summed in bfloat16 or wider, within the bound.
A program may use at most 64 MiB of HBM per device.

v0:
```python
import math

import jax
import jax.numpy as jnp
from jax import lax
from jax.sharding import PartitionSpec as P

HEADS = 24
PATCH = 1024


def contract(left_op, right_op, left_dim, right_dim):
    return lax.dot_general(
        left_op,
        right_op,
        (((left_dim,), (right_dim,)), ((), ())),
        preferred_element_type=jnp.float32,
    )


def head_pass(query_rows, key_rows, value_rows, grad_slice):
    score_scale = query_rows.shape[1] ** (-0.5)
    scores = contract(query_rows, key_rows, 1, 1) * score_scale
    shifted = jnp.exp(scores - jnp.max(scores, axis=1, keepdims=True))
    prob_full = shifted / jnp.sum(shifted, axis=1, keepdims=True)
    prob_low = prob_full.astype(jnp.bfloat16)
    attended = jnp.dot(prob_low, value_rows, preferred_element_type=jnp.float32).astype(
        jnp.bfloat16
    )
    dprobs = contract(grad_slice, value_rows, 1, 1)
    dscores = (
        prob_full * (dprobs - jnp.sum(dprobs * prob_full, axis=1, keepdims=True)) * score_scale
    ).astype(jnp.bfloat16)
    dquery = jnp.dot(dscores, key_rows, preferred_element_type=jnp.float32).astype(jnp.bfloat16)
    dkey_rows = contract(dscores, query_rows, 0, 0).astype(jnp.bfloat16)
    dvalue = contract(prob_low, grad_slice, 0, 0).astype(jnp.bfloat16)
    return (attended, dquery, dkey_rows, dvalue)


def patch_pass(block_rows, block_grads, w_qkv, w_proj, head_count):
    feat_width = block_rows.shape[1]
    head_dim = feat_width // head_count
    values = block_rows.astype(jnp.float32)
    row_mean = jnp.mean(values, axis=1, keepdims=True)
    centred = values - row_mean
    inv_std = lax.rsqrt(jnp.mean(centred * centred, axis=1, keepdims=True) + 1e-05)
    normed = centred * inv_std
    normed_low = normed.astype(jnp.bfloat16)
    projected = jnp.dot(normed_low, w_qkv, preferred_element_type=jnp.float32).astype(jnp.bfloat16)
    upstream = contract(block_grads, w_proj, 1, 1).astype(jnp.bfloat16)

    def one_head(head_index):
        head_start = head_index * head_dim
        query_rows = lax.dynamic_slice_in_dim(projected, head_start, head_dim, 1)
        key_rows = lax.dynamic_slice_in_dim(projected, head_start + feat_width, head_dim, 1)
        value_rows = lax.dynamic_slice_in_dim(projected, head_start + 2 * feat_width, head_dim, 1)
        grad_slice = lax.dynamic_slice_in_dim(upstream, head_start, head_dim, 1)
        return head_pass(query_rows, key_rows, value_rows, grad_slice)

    heads_out = lax.map(one_head, jnp.arange(head_count, dtype=jnp.int32))

    def merge_heads(stacked):
        return jnp.transpose(stacked, (1, 0, 2)).reshape(stacked.shape[1], feat_width)

    attended = merge_heads(heads_out[0])
    dprojected = jnp.concatenate(
        [merge_heads(heads_out[1]), merge_heads(heads_out[2]), merge_heads(heads_out[3])], axis=1
    )
    mixed_out = jnp.dot(attended, w_proj, preferred_element_type=jnp.float32)
    output = (values + mixed_out).astype(jnp.bfloat16)
    dnormed = contract(dprojected, w_qkv, 1, 1)
    dnorm_mean = jnp.mean(dnormed, axis=1, keepdims=True)
    cross_mean = jnp.mean(dnormed * normed, axis=1, keepdims=True)
    dinput = inv_std * (dnormed - dnorm_mean - normed * cross_mean)
    grad_input = (block_grads.astype(jnp.float32) + dinput).astype(jnp.bfloat16)
    return (output, grad_input, normed_low, dprojected, attended)


def on_device(features, cotangent, hilbert_rank, w_qkv, w_proj):
    row_count = features.shape[0]
    feat_width = features.shape[1]
    size_x = lax.axis_size("sx")
    size_y = lax.axis_size("sy")
    devices = size_x * size_y
    capacity = 2 * row_count // devices
    slot_total = devices * capacity
    owner_dev = hilbert_rank // row_count
    place_row = hilbert_rank % row_count
    sort_order = jnp.argsort(hilbert_rank)
    owner_sorted = owner_dev[sort_order]
    labels = jnp.arange(devices, dtype=jnp.int32)
    counts = jnp.sum((owner_dev[:, None] == labels[None, :]).astype(jnp.int32), axis=0)
    starts = jnp.cumsum(counts) - counts
    first_slot = jnp.sum(
        jnp.where(owner_sorted[:, None] == labels[None, :], starts[None, :], 0), axis=1
    )
    slot_sorted = owner_sorted * capacity + jnp.arange(row_count, dtype=jnp.int32) - first_slot
    slot_index = jnp.zeros((row_count,), jnp.int32).at[sort_order].set(slot_sorted)
    send_rows = jnp.zeros((slot_total, feat_width), features.dtype).at[slot_index].set(features)
    send_grads = jnp.zeros((slot_total, feat_width), cotangent.dtype).at[slot_index].set(cotangent)
    send_place = jnp.full((slot_total,), row_count, jnp.int32).at[slot_index].set(place_row)
    got_rows, got_grads, got_place = (
        lax.all_to_all(send_rows, ("sx", "sy"), split_axis=0, concat_axis=0, tiled=True),
        lax.all_to_all(send_grads, ("sx", "sy"), split_axis=0, concat_axis=0, tiled=True),
        lax.all_to_all(send_place, ("sx", "sy"), split_axis=0, concat_axis=0, tiled=True),
    )
    curve_rows = (
        jnp.zeros((row_count, feat_width), jnp.bfloat16).at[got_place].set(got_rows, mode="drop")
    )
    curve_grads = (
        jnp.zeros((row_count, feat_width), jnp.bfloat16).at[got_place].set(got_grads, mode="drop")
    )
    patch_total = row_count // PATCH

    def run_patch(both_blocks):
        return patch_pass(both_blocks[0], both_blocks[1], w_qkv, w_proj, HEADS)

    results = lax.map(
        run_patch,
        (
            curve_rows.reshape(patch_total, PATCH, feat_width),
            curve_grads.reshape(patch_total, PATCH, feat_width),
        ),
    )
    curve_out = results[0].reshape(row_count, feat_width)
    curve_grad = results[1].reshape(row_count, feat_width)
    normed_low = results[2].reshape(row_count, feat_width)
    dprojected = results[3].reshape(row_count, 3 * feat_width)
    attended = results[4].reshape(row_count, feat_width)
    grad_terms = (contract(normed_low, dprojected, 0, 0), contract(attended, curve_grads, 0, 0))
    back_place = jnp.minimum(got_place, row_count - 1)
    back_rows = curve_out[back_place]
    back_grads = curve_grad[back_place]
    ret_rows, ret_grads = (
        lax.all_to_all(back_rows, ("sx", "sy"), split_axis=0, concat_axis=0, tiled=True),
        lax.all_to_all(back_grads, ("sx", "sy"), split_axis=0, concat_axis=0, tiled=True),
    )
    grad_sums = lax.psum((grad_terms[0], grad_terms[1]), ("sx", "sy"))
    grad_scale = 1.0 / math.sqrt(row_count * devices)
    return (
        ret_rows[slot_index],
        ret_grads[slot_index],
        grad_sums[0] * grad_scale,
        grad_sums[1] * grad_scale,
    )


def solution(mesh):
    in_specs = (P(("sx", "sy"), None), P(("sx", "sy"), None), P(("sx", "sy")), P(), P())
    out_specs = (P(("sx", "sy"), None), P(("sx", "sy"), None), P(), P())
    return jax.shard_map(
        on_device, mesh=mesh, in_specs=in_specs, out_specs=out_specs, check_vma=False
    )
```

profile of v0, /device:TPU:1, one launch (start us, length us, event | category | flops | bytes accessed | tf_op | source)
XLA Modules:
  0.0 736.6 jit_solution(12952684937199685522)
XLA Ops:
  7.2 5.1 sort.17
  13.2 4.5 gather_fusion
  18.6 4.3 scatter_custom_fusion
  22.9 4.3 scatter_custom_fusion.1
  27.9 11.5 %all-to-all-start = ((s32[128,16,1]{1,2,0:T(1,128)}), s32[128,16,1]{1,2,0:T(1,128)S(1)}, u32[]{:S(2)}, u32[]{:S(2)}) async-start(s32[128,16,1]{1,2,0:T(1,128)} %bitcast.6), calls=%async_computation | async-start | bytes 131072 | tf_op jit(solution)/shard_map/all_to_all | solution.py:105
  39.4 6.8 scatter_custom_fusion.2
  49.8 6.8 all-to-all-start.1
  56.6 6.8 scatter_custom_fusion.4
  63.4 17.3 %all-to-all-done.1 = bf16[128,16,384]{2,1,0:T(8,128)(2,1)S(1)} async-done(((bf16[128,16,384]{2,1,0:T(8,128)(2,1)}), bf16[128,16,384]{2,1,0:T(8,128)(2,1)S(1)}, u32[]{:S(2)}, u32[]{:S(2)}) %all-to-all-start.1) | async-done | bytes 1572896 | tf_op jit(solution)/shard_map/all_to_all | solution.py:103
  81.8 4.9 all-to-all-start.2
  89.6 9.9 %scatter_custom_fusion.3 = bf16[1024,384]{1,0:T(8,128)(2,1)S(1)} fusion(s32[2048]{0:T(1024)} %bitcast.80, bf16[2048,384]{1,0:T(8,128)(2,1)} %bitcast.76, bf16[]{:T(256)} %constant.129.clone.1), kind=kCustom, calls=%fused_computation.78 | custom fusion | bytes 786944 | tf_op jit(solution)/shard_map/scatter | solution.py:108
  100.9 10.0 %all-to-all-done.2 = bf16[128,16,384]{2,1,0:T(8,128)(2,1)S(1)} async-done(((bf16[128,16,384]{2,1,0:T(8,128)(2,1)}), bf16[128,16,384]{2,1,0:T(8,128)(2,1)S(1)}, u32[]{:S(2)}, u32[]{:S(2)}) %all-to-all-start.2) | async-done | bytes 1572896 | tf_op jit(solution)/shard_map/all_to_all | solution.py:104
  112.1 9.9 %scatter_custom_fusion.5 = bf16[1024,384]{1,0:T(8,128)(2,1)S(1)} fusion(s32[2048]{0:T(1024)} %bitcast.81, bf16[2048,384]{1,0:T(8,128)(2,1)} %bitcast.75, bf16[]{:T(256)} %constant.129.clone.1), kind=kCustom, calls=%fused_computation.76 | custom fusion | bytes 786944 | tf_op jit(solution)/shard_map/scatter | solution.py:111
  122.7 3.7 convolution_convert_fusion.4
  126.9 391.0 %while.32 = (s32[]{:T(128)}, bf16[24,1024,16]{1,2,0:T(8,128)(2,1)}, bf16[24,1024,16]{1,2,0:T(8,128)(2,1)}, bf16[24,1024,16]{1,2,0:T(8,128)(2,1)}, bf16[24,1024,1...) while((s32[]{:T(128)}, bf16[24,1024,16]{1,2,0:T(8,128)(2,1)}, ...), condition=%wide.region_16.17_spmd, body=%wide.region_12.16_spmd.sunk | while | flops 227603472 | bytes 42127728 | solution.py:60
  519.7 9.0 %gather_fusion.1 = bf16[2048,384]{1,0:T(8,128)(2,1)} fusion(bf16[1024,384]{1,0:T(8,128)(2,1)S(1)} %fusion.41, s32[2048]{0:T(1024)S(1)} %broadcast_clamp_fusion), kind=kCustom, calls=%fused_computation.1 | custom fusion | bytes 3153920 | tf_op jit(solution)/shard_map/gather | solution.py:132
  528.8 5.0 all-to-all-start.3
  534.1 3.7 fusion.62
  543.8 3.9 fusion.42
  551.8 9.0 %gather_fusion.3 = bf16[2048,384]{1,0:T(8,128)(2,1)} fusion(bf16[1024,384]{1,0:T(8,128)(2,1)S(1)} %fusion.39, s32[2048]{0:T(1024)S(1)} %broadcast_clamp_fusion), kind=kCustom, calls=%fused_computation.3 | custom fusion | bytes 3153920 | tf_op jit(solution)/shard_map/gather | solution.py:133
  560.8 10.3 %all-to-all-start.4 = ((bf16[128,16,384]{2,1,0:T(8,128)(2,1)}), bf16[128,16,384]{2,1,0:T(8,128)(2,1)}, u32[]{:S(2)}, u32[]{:S(2)}) async-start(bf16[128,16,384]{2,1,0:T(8,128)(2,1)} %bitcast.74), calls=%async_computation.4 | async-start | bytes 3145728 | tf_op jit(solution)/shard_map/all_to_all | solution.py:136
  571.1 142.4 %all-reduce.3.cloned.1.call-done = (f32[384,1152]{1,0:T(8,128)}, f32[384,384]{1,0:T(8,128)}) async-done(((f32[384,1152]{1,0:T(8,128)}, f32[384,384]{1,0:T(8,128)}), (f32[384,1152]{1,0:T(8,128)}, f32[384,384]{1,0:T(8,128)})) %all-reduce.3.cloned.1.call-update) | async-done | bytes 2359312 | tf_op jit(solution)/shard_map/psum | solution.py:138
  718.3 5.0 gather_fusion.2
  723.3 6.5 gather_fusion.4
  (284 shorter events, 404.8 us)
Async XLA Ops:
  7.2 115.5 %copy-start = (bf16[384,1152]{1,0:T(8,128)(2,1)S(1)}, bf16[384,1152]{1,0:T(8,128)(2,1)}, u32[]{:S(2)}) copy-start(bf16[384,1152]{1,0:T(8,128)(2,1)} %param.10) | copy-start | bytes 2654212
  27.9 21.2 %all-to-all-start = ((s32[128,16,1]{1,2,0:T(1,128)}), s32[128,16,1]{1,2,0:T(1,128)S(1)}, u32[]{:S(2)}, u32[]{:S(2)}) async-start(s32[128,16,1]{1,2,0:T(1,128)} %bitcast.6), calls=%async_computation | async-start | bytes 131072 | tf_op jit(solution)/shard_map/all_to_all | solution.py:105
  49.1 0.6 copy-start.9
  49.8 30.9 %all-to-all-start.1 = ((bf16[128,16,384]{2,1,0:T(8,128)(2,1)}), bf16[128,16,384]{2,1,0:T(8,128)(2,1)S(1)}, u32[]{:S(2)}, u32[]{:S(2)}) async-start(bf16[128,16,384]{2,1,0:T(8,128)(2,1)} %bitcast.8), calls=%async_computation.1 | async-start | bytes 3145728 | tf_op jit(solution)/shard_map/all_to_all | solution.py:103
  80.7 1.1 copy-start.7
  81.8 29.1 %all-to-all-start.2 = ((bf16[128,16,384]{2,1,0:T(8,128)(2,1)}), bf16[128,16,384]{2,1,0:T(8,128)(2,1)S(1)}, u32[]{:S(2)}, u32[]{:S(2)}) async-start(bf16[128,16,384]{2,1,0:T(8,128)(2,1)} %bitcast.10), calls=%async_computation.2 | async-start | bytes 3145728 | tf_op jit(solution)/shard_map/all_to_all | solution.py:104
  86.7 35.3 %copy-start.8 = (bf16[384,384]{1,0:T(8,128)(2,1)S(1)}, bf16[384,384]{1,0:T(8,128)(2,1)}, u32[]{:S(2)}) copy-start(bf16[384,384]{1,0:T(8,128)(2,1)} %param.11) | copy-start | bytes 884740
  99.6 418.3 %copy-start.1 = (bf16[1024,384]{1,0:T(8,128)(2,1)}, bf16[1024,384]{1,0:T(8,128)(2,1)S(1)}, u32[]{:S(2)}) copy-start(bf16[1024,384]{1,0:T(8,128)(2,1)S(1)} %scatter_custom_fusion.3) | copy-start | bytes 2359300
  110.9 1.1 copy-start.6
  122.0 4.3 copy-start.5
  528.8 5.3 copy-start.11
  528.8 32.0 %all-to-all-start.3 = ((bf16[128,16,384]{2,1,0:T(8,128)(2,1)}), bf16[128,16,384]{2,1,0:T(8,128)(2,1)S(1)}, u32[]{:S(2)}, u32[]{:S(2)}) async-start(bf16[128,16,384]{2,1,0:T(8,128)(2,1)} %bitcast.73), calls=%async_computation.3 | async-start | bytes 3145728 | tf_op jit(solution)/shard_map/all_to_all | solution.py:135
  533.8 179.7 %all-reduce.3.cloned.1.call-start = ((), (), s32[]{:S(2)}) async-start(), calls=%async_computation.5 | async-start | bytes 4718592 | tf_op jit(solution)/shard_map/psum | solution.py:138
  537.8 6.0 copy-start.2
  537.8 6.0 copy-start.10
  540.9 2.9 copy-start.12
  540.9 2.9 copy-start.13
  547.8 2.1 copy-start.3
  547.8 2.1 copy-start.4
  560.8 162.5 %all-to-all-start.4 = ((bf16[128,16,384]{2,1,0:T(8,128)(2,1)}), bf16[128,16,384]{2,1,0:T(8,128)(2,1)}, u32[]{:S(2)}, u32[]{:S(2)}) async-start(bf16[128,16,384]{2,1,0:T(8,128)(2,1)} %bitcast.74), calls=%async_computation.4 | async-start | bytes 3145728 | tf_op jit(solution)/shard_map/all_to_all | solution.py:136
Sparse Core Ops, SparseCore 0:
  547.9 165.5 all-reduce.2
where the time goes:
time: 741 us; the launch traced here: 737 us
  matrix products  314 us (42%)
  waiting for transfers between devices  173 us (23%)
  local copies, waits for them, and re-layouts  114 us (15%)
  other arithmetic  66.6 us (9%)
  starting transfers between devices  38.8 us (5%)
  loops' own time  16.7 us (2%)
  between operations  14.4 us (2%)
    dot_general x100, matrix products, contract(): lax.dot_general(left_op, right_op, (((left_dim,), (right_dim,)), ((), ())...  199 us
    psum x1, waiting for transfers between devices, on_device(): grad_sums = lax.psum((grad_terms[0], grad_terms[1]), ('sx', 'sy'))  142 us
    dot_general x24, matrix products, head_pass(): jnp.dot(prob_low, value_rows, preferred_element_type=jnp.float32)  59.7 us
    dot_general x24, matrix products, head_pass(): jnp.dot(dscores, key_rows, preferred_element_type=jnp.float32)  49.5 us
    convert_element_type x24, other arithmetic, head_pass(): dscores = (prob_full * (dprobs - jnp.sum(dprobs * prob_full, axis=1, keep...  30.2 us
    dynamic_slice x24, local copies, waits for them, and re-layouts, patch_pass(): heads_out = lax.map(one_head, jnp.arange(head_count, dtype=jnp.int32))  29.7 us
    scatter x2, local copies, waits for them, and re-layouts, on_device(): jnp.zeros((row_count, feat_width), jnp.bfloat16).at[got_place]  19.9 us
    reduce_sum x24, other arithmetic, head_pass(): prob_full = shifted / jnp.sum(shifted, axis=1, keepdims=True)  17.5 us
  transfers between devices with their start and end apart: 6, of which 4 were waited for; matrix products, arithmetic and copies ran while one was open for 9% of the time, Pallas kernels for 0%

commit v1 on v0

v1 whole, which is shorter than its diff:
```python
import functools
import math

import jax
import jax.numpy as jnp
from jax import lax
from jax.experimental import pallas as pl
from jax.experimental.pallas import tpu as pltpu
from jax.sharding import PartitionSpec as P

BF = jnp.bfloat16
F32 = jnp.float32
HEADS = 24
ROWS = 1024
C = 384
DEV = 128
CAP = 16
SLOTS = DEV * CAP
EXT = 2 * C + 128
RC = 256
NR = ROWS // RC
SC = 256
VM = pl.BlockSpec(memory_space=pltpu.VMEM)
PARAMS = pltpu.CompilerParams(vmem_limit_bytes=60 * 1024 * 1024)


def dg(a, b, da, db):
    return lax.dot_general(a, b, (((da,), (db,)), ((), ())), preferred_element_type=F32)


def chunk(i, size):
    return pl.ds(pl.multiple_of(i * size, size), size)


def pack_kernel(x_ref, ct_ref, rank_ref, send_ref, slot_ref, rows):
    rank = jnp.concatenate([rank_ref[i : i + 1, :] for i in range(ROWS // 128)], axis=1)
    owner = rank // ROWS
    place = rank - owner * ROWS
    onehot = lax.broadcasted_iota(jnp.int32, (DEV, ROWS), 0) == owner
    before = (
        lax.broadcasted_iota(jnp.int32, (ROWS, ROWS), 0)
        < lax.broadcasted_iota(jnp.int32, (ROWS, ROWS), 1)
    )
    counts = jnp.dot(
        onehot.astype(F32).astype(BF), before.astype(F32).astype(BF), preferred_element_type=F32
    )
    earlier = jnp.sum(jnp.where(onehot, counts, 0.0), axis=0, keepdims=True)
    slot = owner * CAP + earlier.astype(jnp.int32)
    slot_ref[...] = jnp.broadcast_to(slot, slot_ref.shape)
    high = place // 32
    low = place - high * 32
    line = lax.broadcasted_iota(jnp.int32, (128, ROWS), 0)
    code = jnp.where(line == 0, high + 1, jnp.where(line == 1, low, 0)).astype(F32)
    rows[:, :C] = x_ref[...]
    rows[:, C : 2 * C] = ct_ref[...]
    rows[:, 2 * C :] = code.T.astype(BF)

    def step(i, _):
        pick = (lax.broadcasted_iota(jnp.int32, (SC, ROWS), 0) + i * SC) == slot
        send_ref[chunk(i, SC), :] = jnp.dot(
            pick.astype(F32).astype(BF), rows[...], preferred_element_type=F32
        ).astype(BF)
        return 0

    lax.fori_loop(0, SLOTS // SC, step, 0)


def last_kernel(ret_ref, slot_ref, out_ref, gx_ref, col):
    col[...] = jnp.broadcast_to(slot_ref[0:1, :].astype(F32), (128, ROWS)).T

    def step(i, _):
        rs = chunk(i, RC)
        ids = lax.broadcasted_iota(jnp.int32, (RC, SLOTS), 1).astype(F32)
        pick = (ids == col[rs, 0:1]).astype(F32).astype(BF)
        got = jnp.dot(pick, ret_ref[...], preferred_element_type=F32).astype(BF)
        out_ref[rs, :] = got[:, :C]
        gx_ref[rs, :] = got[:, C:]
        return 0

    lax.fori_loop(0, NR, step, 0)


def layer_norm(rows):
    v = rows.astype(F32)
    c = v - jnp.mean(v, axis=1, keepdims=True)
    inv = lax.rsqrt(jnp.mean(c * c, axis=1, keepdims=True) + 1e-5)
    return v, c * inv, inv


def patch_kernel(
    got_ref, wqkv_ref, wproj_ref, back_ref, gq_ref, gp_ref,
    rows, results, place_row, proj, up, proj_t, up_t, oacc, dqacc, dk_t, dv_t, low, dproj, att,
):
    def places(i, _):
        code = got_ref[chunk(i, SC), 2 * C :].astype(F32)
        t = code.T
        place_row[0:1, chunk(i, SC)] = (t[0:1, :] - 1.0) * 32.0 + t[1:2, :]
        return 0

    lax.fori_loop(0, SLOTS // SC, places, 0)

    def prologue(r, _):
        rs = chunk(r, RC)
        ids = (lax.broadcasted_iota(jnp.int32, (RC, SLOTS), 0) + r * RC).astype(F32)
        pick = (ids == place_row[0:1, :]).astype(F32).astype(BF)
        both = jnp.dot(pick, got_ref[:, : 2 * C], preferred_element_type=F32).astype(BF)
        rows[rs, :] = both
        _, n, _ = layer_norm(both[:, :C])
        nl = n.astype(BF)
        low[rs, :] = nl
        p = jnp.dot(nl, wqkv_ref[...], preferred_element_type=F32).astype(BF)
        u = dg(both[:, C:], wproj_ref[...], 1, 1).astype(BF)
        for g in range(9):
            blk = p[:, g * 128 : (g + 1) * 128]
            proj[g, rs, :] = blk
            if g < 3:
                proj_t[g * 128 : (g + 1) * 128, rs] = (blk * BF(0.25)).T
        for g in range(3):
            blk = u[:, g * 128 : (g + 1) * 128]
            up[g, rs, :] = blk
            up_t[g * 128 : (g + 1) * 128, rs] = blk.T
        return 0

    lax.fori_loop(0, NR, prologue, 0)
    oacc[...] = jnp.zeros_like(oacc)
    dqacc[...] = jnp.zeros_like(dqacc)
    lane = lax.broadcasted_iota(jnp.int32, (1, 128), 1) // 16

    def head(h, _):
        g = h // 8
        mask = (lane == (h - g * 8)).astype(F32).astype(BF)
        k = proj[3 + g]
        v = proj[6 + g]
        km = k * (mask * BF(0.25))
        vm = v * mask
        hs = chunk(h, 16)
        dk = jnp.zeros((16, ROWS), F32)
        dv = jnp.zeros((16, ROWS), F32)
        for r in range(NR):
            rs = slice(r * RC, (r + 1) * RC)
            qm = proj[g, rs, :] * (mask * BF(0.25))
            um = up[g, rs, :] * mask
            s = dg(qm, k, 1, 1)
            dp = dg(um, v, 1, 1)
            e = jnp.exp(s - jnp.max(s, axis=1, keepdims=True))
            linv = 1.0 / jnp.sum(e, axis=1, keepdims=True)
            mid = jnp.sum(e * dp, axis=1, keepdims=True) * linv
            p = e * linv
            pb = p.astype(BF)
            ds = (p * (dp - mid)).astype(BF)
            oacc[g, rs, :] += jnp.dot(pb, vm, preferred_element_type=F32)
            dqacc[g, rs, :] += jnp.dot(ds, km, preferred_element_type=F32)
            dk = dk + jnp.dot(proj_t[hs, rs], ds, preferred_element_type=F32)
            dv = dv + jnp.dot(up_t[hs, rs], pb, preferred_element_type=F32)
        dk_t[hs, :] = dk.astype(BF)
        dv_t[hs, :] = dv.astype(BF)
        return 0

    lax.fori_loop(0, HEADS, head, 0)
    gq_ref[...] = jnp.zeros_like(gq_ref)
    gp_ref[...] = jnp.zeros_like(gp_ref)

    def epilogue(r, _):
        rs = chunk(r, RC)
        v, n, inv = layer_norm(rows[rs, :C])
        for g in range(3):
            att[rs, g * 128 : (g + 1) * 128] = oacc[g, rs, :].astype(BF)
            dproj[rs, g * 128 : (g + 1) * 128] = dqacc[g, rs, :].astype(BF)
        dproj[rs, C : 2 * C] = dk_t[:, rs].T
        dproj[rs, 2 * C :] = dv_t[:, rs].T
        a = att[rs, :]
        dpj = dproj[rs, :]
        ct = rows[rs, C:]
        results[rs, :C] = (v + jnp.dot(a, wproj_ref[...], preferred_element_type=F32)).astype(BF)
        dn = dg(dpj, wqkv_ref[...], 1, 1)
        dm = jnp.mean(dn, axis=1, keepdims=True)
        cm = jnp.mean(dn * n, axis=1, keepdims=True)
        results[rs, C:] = (ct.astype(F32) + inv * (dn - dm - n * cm)).astype(BF)
        gq_ref[...] += dg(low[rs, :], dpj, 0, 0)
        gp_ref[...] += dg(a, ct, 0, 0)
        return 0

    lax.fori_loop(0, NR, epilogue, 0)

    def back(i, _):
        ss = chunk(i, SC)
        code = got_ref[ss, 2 * C :].astype(F32)
        place = (code[:, 0:1] - 1.0) * 32.0 + code[:, 1:2]
        ids = lax.broadcasted_iota(jnp.int32, (SC, ROWS), 1).astype(F32)
        pick = (ids == place).astype(F32).astype(BF)
        back_ref[ss, :] = jnp.dot(pick, results[...], preferred_element_type=F32).astype(BF)
        return 0

    lax.fori_loop(0, SLOTS // SC, back, 0)


def on_device(features, cotangent, hilbert_rank, w_qkv, w_proj):
    shape = jax.ShapeDtypeStruct
    send, slot = pl.pallas_call(
        pack_kernel,
        out_shape=(shape((SLOTS, EXT), BF), shape((8, ROWS), jnp.int32)),
        in_specs=[VM] * 3,
        out_specs=(VM,) * 2,
        scratch_shapes=[pltpu.VMEM((ROWS, EXT), BF)],
        compiler_params=PARAMS,
        name="pack",
    )(features, cotangent, hilbert_rank.reshape(ROWS // 128, 128))
    got = lax.all_to_all(
        send.reshape(DEV, CAP, EXT), ("sx", "sy"), split_axis=0, concat_axis=0, tiled=True
    ).reshape(SLOTS, EXT)
    back, grad_qkv, grad_proj = pl.pallas_call(
        patch_kernel,
        out_shape=(shape((SLOTS, 2 * C), BF), shape((C, 3 * C), F32), shape((C, C), F32)),
        in_specs=[VM] * 3,
        out_specs=(VM,) * 3,
        scratch_shapes=[
            pltpu.VMEM((ROWS, 2 * C), BF),
            pltpu.VMEM((ROWS, 2 * C), BF),
            pltpu.VMEM((8, SLOTS), F32),
            pltpu.VMEM((9, ROWS, 128), BF),
            pltpu.VMEM((3, ROWS, 128), BF),
            pltpu.VMEM((C, ROWS), BF),
            pltpu.VMEM((C, ROWS), BF),
            pltpu.VMEM((3, ROWS, 128), F32),
            pltpu.VMEM((3, ROWS, 128), F32),
            pltpu.VMEM((C, ROWS), BF),
            pltpu.VMEM((C, ROWS), BF),
            pltpu.VMEM((ROWS, C), BF),
            pltpu.VMEM((ROWS, 3 * C), BF),
            pltpu.VMEM((ROWS, C), BF),
        ],
        compiler_params=PARAMS,
        name="patch",
    )(got, w_qkv, w_proj)
    ret = lax.all_to_all(
        back.reshape(DEV, CAP, 2 * C), ("sx", "sy"), split_axis=0, concat_axis=0, tiled=True
    ).reshape(SLOTS, 2 * C)
    sums = lax.psum((grad_qkv, grad_proj), ("sx", "sy"))
    scale = 1.0 / math.sqrt(ROWS * DEV)
    outputs, grad_features = pl.pallas_call(
        last_kernel,
        out_shape=(shape((ROWS, C), BF), shape((ROWS, C), BF)),
        in_specs=[VM] * 2,
        out_specs=(VM,) * 2,
        scratch_shapes=[pltpu.VMEM((ROWS, 128), F32)],
        compiler_params=PARAMS,
        name="last",
    )(ret, slot)
    return outputs, grad_features, sums[0] * scale, sums[1] * scale


def solution(mesh):
    in_specs = (P(("sx", "sy"), None), P(("sx", "sy"), None), P(("sx", "sy")), P(), P())
    out_specs = (P(("sx", "sy"), None), P(("sx", "sy"), None), P(), P())
    return jax.shard_map(
        on_device, mesh=mesh, in_specs=in_specs, out_specs=out_specs, check_vma=False
    )
```

time: 741 us -> 394 us (0.53)
  matrix products: 314 us -> 0 us
  Pallas kernels: 0 us -> 137 us
  local copies, waits for them, and re-layouts: 114 us -> 1.64 us
  other arithmetic: 66.6 us -> 4.76 us
  blocking collectives: 0 us -> 57.7 us
  starting transfers between devices: 38.8 us -> 4.86 us
  loops' own time: 16.7 us -> 0 us
    dot_general x150 -> x0, matrix products: 314 us -> none  [the longest x100 199 us: contract(): lax.dot_general(left_op, right_op, (((left_dim,), (right_dim,)), ((), ())...]
    pallas_call x0 -> x3, Pallas kernels: none -> 137 us  [the longest x1 120 us: on_device(): pl.pallas_call(patch_kernel, out_shape=(shape((SLOTS, 2 * C), BF), shape(...]
    all_to_all x0 -> x1, blocking collectives: none -> 57.7 us  [on_device(): lax.all_to_all(send.reshape(DEV, CAP, EXT), ('sx', 'sy'), split_axis=0, c...]
    scatter x6 -> x0, local copies, waits for them, and re-layouts: 42.1 us -> none  [the longest x2 19.9 us: on_device(): jnp.zeros((row_count, feat_width), jnp.bfloat16).at[got_place]]
    gather x5 -> x0, local copies, waits for them, and re-layouts: 34.1 us -> none  [the longest x1 9.05 us: on_device(): back_rows = curve_out[back_place]]
    all_to_all x5 -> x1, starting transfers between devices: 38.5 us -> 4.82 us  [on_device(): lax.all_to_all(back.reshape(DEV, CAP, 2 * C), ('sx', 'sy'), split_axis=0,...]
    convert_element_type x25 -> x0, other arithmetic: 32.1 us -> none  [the longest x24 30.2 us: head_pass(): dscores = (prob_full * (dprobs - jnp.sum(dprobs * prob_full, axis=1, keep...]
    all_to_all x5 -> x1, waiting for transfers between devices: 30.3 us -> 0.01 us  [on_device(): lax.all_to_all(back.reshape(DEV, CAP, 2 * C), ('sx', 'sy'), split_axis=0,...]
  transfers between devices with their start and end apart: 6 -> 2, of which waited for: 4 -> 1; matrix products, arithmetic and copies ran while one was open for 9% -> 1% of each run, Pallas kernels for 0% -> 0%
where the time goes in v1:
time: 394 us; the launch traced here: 393 us
  waiting for transfers between devices  173 us (44%)
  Pallas kernels  137 us (35%)
  blocking collectives  57.7 us (15%)
  between operations  14 us (4%)
  starting transfers between devices  4.86 us (1%)
  other arithmetic  4.76 us (1%)
    psum x1, waiting for transfers between devices, on_device(): sums = lax.psum((grad_qkv, grad_proj), ('sx', 'sy'))  173 us
    pallas_call x1, Pallas kernels, on_device(): pl.pallas_call(patch_kernel, out_shape=(shape((SLOTS, 2 * C), BF), shape(...  120 us
    all_to_all x1, blocking collectives, on_device(): lax.all_to_all(send.reshape(DEV, CAP, EXT), ('sx', 'sy'), split_axis=0, c...  57.7 us
    pallas_call x1, Pallas kernels, on_device(): pl.pallas_call(pack_kernel, out_shape=(shape((SLOTS, EXT), BF), shape((8,...  9.5 us
  transfers between devices with their start and end apart: 2, of which 1 were waited for; matrix products, arithmetic and copies ran while one was open for 1% of the time, Pallas kernels for 0%

profile of v1, /device:TPU:1, one launch (start us, length us, event | category | flops | bytes accessed | tf_op | source)
XLA Modules:
  0.0 393.5 jit_solution(14511110372182978385)
XLA Ops:
  7.2 9.5 %pack.1 = (bf16[2048,896]{1,0:T(8,128)(2,1)}, s32[8,1024]{1,0:T(8,128)}) custom-call(bf16[1024,384]{1,0:T(8,128)(2,1)} %x_ref.1, bf16[1024,384]{1,0:T(8,128)(2,1)} %ct_ref.1, s32[8,128]{1,0:T(8,128)} %bitcast.9), custom_call_target="tpu_custom_call" | custom-call | tf_op jit(solution)/shard_map/pack/pallas_call | solution.py:199
  16.7 57.7 %all_to_all.10 = bf16[128,16,896]{2,1,0:T(8,128)(2,1)} all-to-all(bf16[128,16,896]{2,1,0:T(8,128)(2,1)} %bitcast.7), channel_id=1, replica_groups=mesh['sx'=8,'sy'=16] {'sx','sy'}, dimensions={0} | all-to-all | bytes 7340032 | tf_op jit(solution)/shard_map/all_to_all | solution.py:208
  74.4 120.3 %patch.1 = (bf16[2048,768]{1,0:T(8,128)(2,1)}, f32[384,1152]{1,0:T(8,128)}, f32[384,384]{1,0:T(8,128)}) custom-call(bf16[2048,896]{1,0:T(8,128)(2,1)} %bitcast.5, bf16[384,1152]{1,0:T(8,128)(2,1)} %wqkv_ref.1, bf16[384,384]{1,0:T(8,128)(2,1)} %wproj_ref.1), custom_call_target="tpu_custom_call" | custom-call | tf_op jit(solution)/shard_map/patch/pallas_call | solution.py:211
  194.7 4.8 %all-to-all-start.1 = ((bf16[128,16,768]{2,1,0:T(8,128)(2,1)}), bf16[128,16,768]{2,1,0:T(8,128)(2,1)S(1)}, u32[]{:S(2)}, u32[]{:S(2)}) async-start(bf16[128,16,768]{2,1,0:T(8,128)(2,1)} %bitcast.8), calls=%async_computation.1 | async-start | bytes 6291456 | tf_op jit(solution)/shard_map/all_to_all | solution.py:235
  199.5 0.0 all-reduce.3.cloned.1.call-start
  199.6 0.7 all-reduce.3.cloned.1.call-update
  200.2 172.6 %all-reduce.3.cloned.1.call-done = (f32[384,1152]{1,0:T(8,128)}, f32[384,384]{1,0:T(8,128)}) async-done(((f32[384,1152]{1,0:T(8,128)}, f32[384,384]{1,0:T(8,128)}), (f32[384,1152]{1,0:T(8,128)}, f32[384,384]{1,0:T(8,128)})) %all-reduce.3.cloned.1.call-update) | async-done | bytes 2359312 | tf_op jit(solution)/shard_map/psum | solution.py:238
  372.9 1.9 broadcast_multiply_fusion.1
  374.8 2.8 broadcast_multiply_fusion
  377.6 0.0 all-to-all-done.1
  377.6 0.0 copy-start
  377.6 1.6 copy-done
  379.3 7.3 %last.1 = (bf16[1024,384]{1,0:T(8,128)(2,1)}, bf16[1024,384]{1,0:T(8,128)(2,1)}) custom-call(bf16[2048,768]{1,0:T(8,128)(2,1)} %bitcast.6, s32[8,1024]{1,0:T(8,128)} %get-tuple-element.13.slot_ref), custom_call_target="tpu_custom_call" | custom-call | tf_op jit(solution)/shard_map/last/pallas_call | solution.py:240
Async XLA Ops:
  194.7 182.9 %all-to-all-start.1 = ((bf16[128,16,768]{2,1,0:T(8,128)(2,1)}), bf16[128,16,768]{2,1,0:T(8,128)(2,1)S(1)}, u32[]{:S(2)}, u32[]{:S(2)}) async-start(bf16[128,16,768]{2,1,0:T(8,128)(2,1)} %bitcast.8), calls=%async_computation.1 | async-start | bytes 6291456 | tf_op jit(solution)/shard_map/all_to_all | solution.py:235
  199.5 173.3 %all-reduce.3.cloned.1.call-start = ((), (), s32[]{:S(2)}) async-start(), calls=%async_computation.2 | async-start | bytes 4718592 | tf_op jit(solution)/shard_map/psum | solution.py:238
  377.6 1.6 copy-start
Sparse Core Ops, SparseCore 0:
  205.8 167.0 all-reduce.2

commit v2 on v1

v2 whole, which is shorter than its diff:
```python
import functools
import math

import jax
import jax.numpy as jnp
from jax import lax
from jax.experimental import pallas as pl
from jax.experimental.pallas import tpu as pltpu
from jax.sharding import PartitionSpec as P

BF = jnp.bfloat16
F32 = jnp.float32
MESH = pl.DeviceIdType.MESH
HEADS = 24
ROWS = 1024
C = 384
NX = 8
NY = 16
DEV = NX * NY
CHIPS = DEV // 2
CAP = 16
SLOTS = DEV * CAP
RC = 256
NR = ROWS // RC
SC = NY * CAP
FIRST = (0, 3072, 24)
SECOND = (3072, 2048, 16)
GROWS = FIRST[1] + SECOND[1]
VM = pl.BlockSpec(memory_space=pltpu.VMEM)
ANY = pl.BlockSpec(memory_space=pl.ANY)


def dg(a, b, da, db):
    return lax.dot_general(a, b, (((da,), (db,)), ((), ())), preferred_element_type=F32)


def chunk(i, size):
    return pl.ds(pl.multiple_of(i * size, size), size)


def hot(test):
    return test.astype(F32).astype(BF)


def iota(shape, dim):
    return lax.broadcasted_iota(jnp.int32, shape, dim).astype(F32)


def layer_norm(rows):
    v = rows.astype(F32)
    c = v - jnp.mean(v, axis=1, keepdims=True)
    inv = lax.rsqrt(jnp.mean(c * c, axis=1, keepdims=True) + 1e-5)
    return v, c * inv, inv


def wait_for(ref, sem):
    pltpu.make_async_copy(ref, ref, sem).wait()


class Reduction:
    def __init__(self, span, terms, total, half, own, part, mine, sem, sx, sy):
        self.base, self.count, self.piece = span
        self.terms, self.total = terms, total
        self.half, self.own, self.part, self.mine, self.sem = half, own, part, mine, sem
        self.core = lax.rem(sx, 2)
        self.chip = (sx // 2) * NY + sy
        self.partner = (sx + 1 - 2 * self.core, sy)

    def side(self, core):
        n = self.count // 2
        return pl.ds(pl.multiple_of(self.base + core * n, 8), n)

    def remote(self, src, dst, i, dev):
        return pltpu.make_async_remote_copy(
            src_ref=src, dst_ref=dst, send_sem=self.sem.at[i], recv_sem=self.sem.at[i + 1],
            device_id=dev, device_id_type=MESH,
        )

    def others(self, start):
        def go(d, _):
            t = lax.rem(self.chip + d, CHIPS)
            start(t, ((t // NY) * 2 + self.core, lax.rem(t, NY)))
            return 0

        lax.fori_loop(1, CHIPS, go, 0)

    def placed(self, t):
        n = self.count // 2
        return pl.ds(pl.multiple_of(self.base + self.core * n + t * self.piece, 8), self.piece)

    def pair(self):
        self.remote(self.terms.at[self.side(1 - self.core)], self.half, 0, self.partner).start()

    def scatter(self):
        wait_for(self.half, self.sem.at[1])
        self.own[...] = self.terms[self.side(self.core), :] + self.half[...]
        self.others(
            lambda t, dev: self.remote(
                self.own.at[chunk(t, self.piece)], self.part.at[chunk(self.chip, self.piece)], 2, dev
            ).start()
        )
        self.part[chunk(self.chip, self.piece), :] = self.own[chunk(self.chip, self.piece), :]

    def gather(self):
        rest = self.part.at[pl.ds(0, (CHIPS - 1) * self.piece)]
        wait_for(rest, self.sem.at[3])

        def add(t, acc):
            return acc + self.part[chunk(t, self.piece), :]

        self.mine[...] = lax.fori_loop(0, CHIPS, add, jnp.zeros((self.piece, 128), F32))
        pltpu.make_async_copy(
            self.mine, self.total.at[self.placed(self.chip)], self.sem.at[8]
        ).start()
        self.others(
            lambda t, dev: self.remote(
                self.mine, self.total.at[self.placed(self.chip)], 4, dev
            ).start()
        )

    def give(self):
        rest = self.part.at[pl.ds(0, (CHIPS - 1) * self.piece)]
        wait_for(rest, self.sem.at[5])
        wait_for(self.mine, self.sem.at[8])
        mine = self.total.at[self.side(self.core)]
        self.remote(mine, mine, 6, self.partner).start()

    def finish(self):
        rest = self.part.at[pl.ds(0, (CHIPS - 1) * self.piece)]
        wait_for(self.half, self.sem.at[7])
        wait_for(self.half, self.sem.at[6])
        wait_for(rest, self.sem.at[4])
        wait_for(rest, self.sem.at[2])
        wait_for(self.half, self.sem.at[0])


def patch_kernel(
    x_ref, ct_ref, rank_ref, wqkv_ref, wproj_ref,
    ret_ref, total_ref, slot_ref,
    send, got, back, place_out, place_in, place_row, pick, rows, results,
    proj, up, proj_t, up_t, oacc, dqacc, dk_t, dv_t, low_t, ct_t, dproj, att, terms,
    half_a, own_a, part_a, mine_a, half_b, own_b, part_b, mine_b, sem_a, sem_b, sem,
):
    sx = lax.axis_index("sx")
    sy = lax.axis_index("sy")
    me = sx * NY + sy
    barrier = pltpu.get_barrier_semaphore()

    def greet(d, _):
        t = lax.rem(me + d, DEV)
        pl.semaphore_signal(barrier, 1, device_id=(t // NY, lax.rem(t, NY)), device_id_type=MESH)
        return 0

    lax.fori_loop(1, DEV, greet, 0)
    sums = (
        Reduction(FIRST, terms, total_ref, half_a, own_a, part_a, mine_a, sem_a, sx, sy),
        Reduction(SECOND, terms, total_ref, half_b, own_b, part_b, mine_b, sem_b, sx, sy),
    )

    def copy_to(src, dst, t, i):
        pltpu.make_async_remote_copy(
            src_ref=src, dst_ref=dst, send_sem=sem.at[i], recv_sem=sem.at[i + 1],
            device_id=(t // NY, lax.rem(t, NY)), device_id_type=MESH,
        ).start()

    def send_part(part, ref, dst, step, i):
        tx = lax.rem(sx + step, NX)

        def go(d, _):
            t = tx * NY + lax.rem(sy + d, NY)
            copy_to(ref.at[part, chunk(t, CAP)], dst.at[part, chunk(me, CAP)], t, i)
            return 0

        lax.fori_loop(jnp.where(step == 0, 1, 0), NY, go, 0)

    rank = jnp.concatenate([rank_ref[i : i + 1, :] for i in range(ROWS // 128)], axis=1)
    owner = rank // ROWS
    place = rank - owner * ROWS
    owned = iota((DEV, ROWS), 0) == owner.astype(F32)
    before = iota((ROWS, ROWS), 0) < iota((ROWS, ROWS), 1)
    counts = jnp.dot(hot(owned), hot(before), preferred_element_type=F32)
    earlier = jnp.sum(jnp.where(owned, counts, 0.0), axis=0, keepdims=True)
    slot = owner.astype(F32) * CAP + earlier
    slot_ref[...] = jnp.broadcast_to(slot, slot_ref.shape)
    high = place // 32
    line = iota((128, ROWS), 0) == earlier
    codes = [
        dg(hot(owned), jnp.where(line, v.astype(F32), 0.0).astype(BF), 1, 1)
        for v in (high + 1, place - high * 32)
    ]
    place_out[...] = (codes[0] * 32.0 + codes[1]).reshape(DEV, 1, 128)
    pl.semaphore_wait(barrier, DEV - 1)

    def packs(part, src):
        def step(k, _):
            tx = lax.rem(sx + k, NX)
            ids = iota((SC, ROWS), 0) + (tx * SC).astype(F32)
            send[part, chunk(tx, SC), :] = jnp.dot(
                hot(ids == slot), src[...], preferred_element_type=F32
            ).astype(BF)

            @pl.when(k > 0)
            def _():
                send_part(part, send, got, k - 1, 2 * part)

            return 0

        lax.fori_loop(0, NX, step, 0)

    packs(0, x_ref)

    def send_place(d, _):
        t = lax.rem(me + d, DEV)
        copy_to(place_out.at[t], place_in.at[me], t, 4)
        return 0

    lax.fori_loop(1, DEV, send_place, 0)
    place_in[me] = place_out[me]
    send_part(0, send, got, NX - 1, 0)
    packs(1, ct_ref)
    send_part(1, send, got, NX - 1, 2)
    mine = chunk(me, CAP)
    got[0, mine, :] = send[0, mine, :]
    got[1, mine, :] = send[1, mine, :]

    wait_for(place_in.at[pl.ds(0, DEV - 1)], sem.at[5])
    code = place_in[...].reshape(DEV, 128).T[0:CAP, :]
    big = jnp.floor(code * (1.0 / 32.0))
    spread = hot(iota((DEV, SLOTS), 0) == jnp.floor(iota((DEV, SLOTS), 1) * (1.0 / CAP)))
    both = [
        jnp.dot(v.astype(BF), spread, preferred_element_type=F32)
        for v in (big, code - big * 32.0)
    ]
    lanes = iota((CAP, SLOTS), 1)
    keep = (lanes - jnp.floor(lanes * (1.0 / CAP)) * CAP) == iota((CAP, SLOTS), 0)
    found = jnp.sum(jnp.where(keep, both[0] * 32.0 + both[1], 0.0), axis=0, keepdims=True)
    place_row[...] = jnp.broadcast_to(found - 32.0, place_row.shape)

    wait_for(got.at[0, pl.ds(0, SLOTS - CAP)], sem.at[1])

    def forward_rows(r, _):
        rs = chunk(r, RC)
        ids = iota((RC, SLOTS), 0) + (r * RC).astype(F32)
        q = hot(ids == place_row[0:1, :])
        pick[rs, :] = q
        x = jnp.dot(q, got[0], preferred_element_type=F32).astype(BF)
        rows[rs, :C] = x
        _, n, _ = layer_norm(x)
        nl = n.astype(BF)
        low_t[:, rs] = nl.T
        p = jnp.dot(nl, wqkv_ref[...], preferred_element_type=F32).astype(BF)
        for g in range(9):
            blk = p[:, g * 128 : (g + 1) * 128]
            proj[g, rs, :] = blk
            if g < 3:
                proj_t[g * 128 : (g + 1) * 128, rs] = (blk * BF(0.25)).T
        return 0

    lax.fori_loop(0, NR, forward_rows, 0)
    oacc[...] = jnp.zeros_like(oacc)
    dqacc[...] = jnp.zeros_like(dqacc)
    terms[GROWS - SECOND[1] + 4 * C :, :] = jnp.zeros((SECOND[1] - 4 * C, 128), F32)
    wait_for(got.at[1, pl.ds(0, SLOTS - CAP)], sem.at[3])

    def upstream_rows(r, _):
        rs = chunk(r, RC)
        ct = jnp.dot(pick[rs, :], got[1], preferred_element_type=F32).astype(BF)
        rows[rs, C:] = ct
        ct_t[:, rs] = ct.T
        u = dg(ct, wproj_ref[...], 1, 1).astype(BF)
        for g in range(3):
            blk = u[:, g * 128 : (g + 1) * 128]
            up[g, rs, :] = blk
            up_t[g * 128 : (g + 1) * 128, rs] = blk.T
        return 0

    lax.fori_loop(0, NR, upstream_rows, 0)
    lane = lax.broadcasted_iota(jnp.int32, (1, 128), 1) // 16

    def head(h, _):
        g = h // 8
        mask = hot(lane == (h - g * 8))
        k = proj[3 + g]
        v = proj[6 + g]
        km = k * (mask * BF(0.25))
        vm = v * mask
        hs = chunk(h, 16)
        dk = jnp.zeros((16, ROWS), F32)
        dv = jnp.zeros((16, ROWS), F32)
        for r in range(NR):
            rs = slice(r * RC, (r + 1) * RC)
            qm = proj[g, rs, :] * (mask * BF(0.25))
            um = up[g, rs, :] * mask
            s = dg(qm, k, 1, 1)
            dp = dg(um, v, 1, 1)
            e = jnp.exp(s - jnp.max(s, axis=1, keepdims=True))
            linv = 1.0 / jnp.sum(e, axis=1, keepdims=True)
            mid = jnp.sum(e * dp, axis=1, keepdims=True) * linv
            p = e * linv
            pb = p.astype(BF)
            ds = (p * (dp - mid)).astype(BF)
            oacc[g, rs, :] += jnp.dot(pb, vm, preferred_element_type=F32)
            dqacc[g, rs, :] += jnp.dot(ds, km, preferred_element_type=F32)
            dk = dk + jnp.dot(proj_t[hs, rs], ds, preferred_element_type=F32)
            dv = dv + jnp.dot(up_t[hs, rs], pb, preferred_element_type=F32)
        dk_t[hs, :] = dk.astype(BF)
        dv_t[hs, :] = dv.astype(BF)

        @pl.when(h == 17)
        def _():
            sums[0].scatter()

        @pl.when(h == 20)
        def _():
            sums[0].gather()

        @pl.when(h == 23)
        def _():
            sums[0].give()

        @pl.when(h - g * 8 == 7)
        def _():
            gs = chunk(g, 128)
            base = g * (4 * C)
            parts = (
                dqacc[g].astype(BF),
                dk_t[gs, :].T,
                dv_t[gs, :].T,
                oacc[g].astype(BF),
            )
            for i, part in enumerate(parts):
                if i < 3:
                    dproj[i, g] = part
                else:
                    att[g] = part
                terms[pl.ds(pl.multiple_of(base + i * C, 128), C), :] = jnp.dot(
                    (ct_t if i == 3 else low_t)[...], part, preferred_element_type=F32
                )

        @pl.when(h == 15)
        def _():
            sums[0].pair()

        return 0

    lax.fori_loop(0, HEADS, head, 0)
    sums[1].pair()

    def epilogue(r, _):
        rs = chunk(r, RC)
        v, n, inv = layer_norm(rows[rs, :C])
        a = jnp.concatenate([att[g, rs, :] for g in range(3)], axis=1)
        dpj = jnp.concatenate([dproj[i, g, rs, :] for i in range(3) for g in range(3)], axis=1)
        ct = rows[rs, C:]
        results[rs, :C] = (v + jnp.dot(a, wproj_ref[...], preferred_element_type=F32)).astype(BF)
        dn = dg(dpj, wqkv_ref[...], 1, 1)
        dm = jnp.mean(dn, axis=1, keepdims=True)
        cm = jnp.mean(dn * n, axis=1, keepdims=True)
        results[rs, C:] = (ct.astype(F32) + inv * (dn - dm - n * cm)).astype(BF)
        return 0

    lax.fori_loop(0, NR, epilogue, 0)
    sums[1].scatter()

    def send_back(step):
        tx = lax.rem(sx + step, NX)

        def go(d, _):
            t = tx * NY + lax.rem(sy + d, NY)
            copy_to(back.at[chunk(t, CAP)], ret_ref.at[chunk(me, CAP)], t, 6)
            return 0

        lax.fori_loop(jnp.where(step == 0, 1, 0), NY, go, 0)

    def backs(k, _):
        tx = lax.rem(sx + k, NX)
        ss = chunk(tx, SC)
        spot = jnp.broadcast_to(place_row[0:1, ss], (128, SC)).T[:, 0:1]
        q = hot(iota((SC, ROWS), 1) == spot)
        back[ss, :] = jnp.dot(q, results[...], preferred_element_type=F32).astype(BF)

        @pl.when(k > 0)
        def _():
            send_back(k - 1)

        return 0

    lax.fori_loop(0, NX // 2, backs, 0)
    sums[1].gather()
    lax.fori_loop(NX // 2, NX, backs, 0)
    send_back(NX - 1)
    own = pltpu.make_async_copy(back.at[mine], ret_ref.at[mine], sem.at[8])
    own.start()
    sums[1].give()
    for part in range(2):
        wait_for(send.at[part, pl.ds(0, SLOTS - CAP)], sem.at[2 * part])
    wait_for(place_out.at[pl.ds(0, DEV - 1)], sem.at[4])
    own.wait()
    for i in range(6, 8):
        wait_for(back.at[pl.ds(0, SLOTS - CAP)], sem.at[i])
    sums[0].finish()
    sums[1].finish()


def last_kernel(scale, ret_ref, slot_ref, total_ref, out_ref, gx_ref, gq_ref, gp_ref, col):
    col[...] = jnp.broadcast_to(slot_ref[0:1, :], (128, ROWS)).T

    def step(i, _):
        rs = chunk(i, RC)
        q = hot(iota((RC, SLOTS), 1) == col[rs, 0:1])
        row = jnp.dot(q, ret_ref[...], preferred_element_type=F32).astype(BF)
        out_ref[rs, :] = row[:, :C]
        gx_ref[rs, :] = row[:, C:]
        return 0

    lax.fori_loop(0, NR, step, 0)
    for g in range(3):
        for i in range(4):
            block = total_ref[(4 * g + i) * C : (4 * g + i + 1) * C, :] * scale
            if i < 3:
                gq_ref[:, i * C + g * 128 : i * C + (g + 1) * 128] = block
            else:
                gp_ref[g * 128 : (g + 1) * 128, :] = block.T


def on_device(features, cotangent, hilbert_rank, w_qkv, w_proj):
    shape = jax.ShapeDtypeStruct
    vm = pltpu.VMEM
    dma = pltpu.SemaphoreType.DMA

    def room(span):
        return [
            vm((span[1] // 2, 128), F32), vm((span[1] // 2, 128), F32),
            vm((span[1] // 2, 128), F32), vm((span[2], 128), F32),
        ]

    ret, total, slot = pl.pallas_call(
        patch_kernel,
        out_shape=(shape((SLOTS, 2 * C), BF), shape((GROWS, 128), F32), shape((8, ROWS), F32)),
        in_specs=[VM] * 5,
        out_specs=(ANY, ANY, VM),
        scratch_shapes=[
            vm((2, SLOTS, C), BF), vm((2, SLOTS, C), BF), vm((SLOTS, 2 * C), BF),
            vm((DEV, 1, 128), F32), vm((DEV, 1, 128), F32), vm((8, SLOTS), F32),
            vm((ROWS, SLOTS), BF), vm((ROWS, 2 * C), BF), vm((ROWS, 2 * C), BF),
            vm((9, ROWS, 128), BF), vm((3, ROWS, 128), BF), vm((C, ROWS), BF), vm((C, ROWS), BF),
            vm((3, ROWS, 128), F32), vm((3, ROWS, 128), F32), vm((C, ROWS), BF), vm((C, ROWS), BF),
            vm((C, ROWS), BF), vm((C, ROWS), BF), vm((3, 3, ROWS, 128), BF), vm((3, ROWS, 128), BF),
            vm((GROWS, 128), F32),
        ] + room(FIRST) + room(SECOND) + [dma((9,)), dma((9,)), dma((9,))],
        compiler_params=pltpu.CompilerParams(
            vmem_limit_bytes=62 * 1024 * 1024, collective_id=0, has_side_effects=True
        ),
        name="patch",
    )(features, cotangent, hilbert_rank.reshape(ROWS // 128, 128), w_qkv, w_proj)
    return pl.pallas_call(
        functools.partial(last_kernel, 1.0 / math.sqrt(ROWS * DEV)),
        out_shape=(
            shape((ROWS, C), BF), shape((ROWS, C), BF), shape((C, 3 * C), F32), shape((C, C), F32),
        ),
        in_specs=[VM] * 3,
        out_specs=(VM,) * 4,
        scratch_shapes=[vm((ROWS, 128), F32)],
        compiler_params=pltpu.CompilerParams(vmem_limit_bytes=60 * 1024 * 1024),
        name="last",
    )(ret, slot, total)


def solution(mesh):
    in_specs = (P(("sx", "sy"), None), P(("sx", "sy"), None), P(("sx", "sy")), P(), P())
    out_specs = (P(("sx", "sy"), None), P(("sx", "sy"), None), P(), P())
    return jax.shard_map(
        on_device, mesh=mesh, in_specs=in_specs, out_specs=out_specs, check_vma=False
    )
```

time: 394 us -> 231 us (0.59)
  waiting for transfers between devices: 173 us -> 0 us
  Pallas kernels: 137 us -> 230 us
  blocking collectives: 57.7 us -> 0 us
  between operations: 14 us -> 0.64 us
  starting transfers between devices: 4.86 us -> 0 us
  other arithmetic: 4.76 us -> 0 us
    psum x1 -> x0, waiting for transfers between devices: 173 us -> none  [on_device(): sums = lax.psum((grad_qkv, grad_proj), ('sx', 'sy'))]
    pallas_call x1, Pallas kernels: 120 us -> 221 us  [on_device(): pl.pallas_call(patch_kernel, out_shape=(shape((SLOTS, 2 * C), BF), shape(...]
    all_to_all x1 -> x0, blocking collectives: 57.7 us -> none  [on_device(): lax.all_to_all(send.reshape(DEV, CAP, EXT), ('sx', 'sy'), split_axis=0, c...]
    pallas_call x2 -> x1, Pallas kernels: 16.8 us -> 8.95 us  [on_device(): pl.pallas_call(functools.partial(last_kernel, 1.0 / math.sqrt(ROWS * DEV)...]
    all_to_all x1 -> x0, starting transfers between devices: 4.82 us -> none  [on_device(): lax.all_to_all(back.reshape(DEV, CAP, 2 * C), ('sx', 'sy'), split_axis=0,...]
    mul x2 -> x0, other arithmetic: 4.76 us -> none  [on_device(): return (outputs, grad_features, sums[0] * scale, sums[1] * scale)]
  transfers between devices with their start and end apart: 2 -> 0, of which waited for: 1 -> 0; matrix products, arithmetic and copies ran while one was open for 1% -> 0% of each run, Pallas kernels for 0% -> 0%
where the time goes in v2:
time: 231 us
  Pallas kernels  230 us (100%)
    pallas_call x1, Pallas kernels, on_device(): pl.pallas_call(patch_kernel, out_shape=(shape((SLOTS, 2 * C), BF), shape(...  221 us
    pallas_call x1, Pallas kernels, on_device(): pl.pallas_call(functools.partial(last_kernel, 1.0 / math.sqrt(ROWS * DEV)...  8.95 us

profile of v2, /device:TPU:1, one launch (start us, length us, event | category | flops | bytes accessed | tf_op | source)
XLA Modules:
  0.0 230.8 jit_solution(4511746456445788278)
XLA Ops:
  0.6 221.2 %patch.1 = (bf16[2048,768]{1,0:T(8,128)(2,1)}, f32[5120,128]{1,0:T(8,128)}, f32[8,1024]{1,0:T(8,128)}) custom-call(bf16[1024,384]{1,0:T(8,128)(2,1)} %x_ref.1, bf16[1024,384]{1,0:T(8,128)(2,1)} %ct_ref.1, s32[8,128]{1,0:T(8,128)} %bitcast.1, bf16[384,1152]{1,0:T(8,128)(2,1)} %wqkv_ref.1, bf16[384,384]{1,0:T(8,128)(2,1)} %wproj_ref.1), custom_call_target="tpu_custom_call" | custom-call | tf_op jit(solution)/shard_map/patch/pallas_call | solution.py:437
  221.8 8.9 %last.1 = (bf16[1024,384]{1,0:T(8,128)(2,1)}, bf16[1024,384]{1,0:T(8,128)(2,1)}, f32[384,1152]{1,0:T(8,128)}, f32[384,384]{1,0:T(8,128)}) custom-call(bf16[2048,768]{1,0:T(8,128)(2,1)} %get-tuple-element.7.ret_ref, f32[8,1024]{1,0:T(8,128)} %get-tuple-element.8.slot_ref, f32[5120,128]{1,0:T(8,128)} %get-tuple-element.9.total_ref), custom_call_target="tpu_custom_call" | custom-call | tf_op jit(solution)/shard_map/last/pallas_call | solution.py:456

commit v3 on v2

--- a/solution.py
+++ b/solution.py
@@ -21,6 +21,7 @@
 CAP = 16
 SLOTS = DEV * CAP
 RC = 256
+HC = 512
 NR = ROWS // RC
 SC = NY * CAP
 FIRST = (0, 3072, 24)
@@ -136,8 +137,8 @@
 
 def patch_kernel(
     x_ref, ct_ref, rank_ref, wqkv_ref, wproj_ref,
-    ret_ref, total_ref, slot_ref,
-    send, got, back, place_out, place_in, place_row, pick, rows, results,
+    out_ref, gx_ref, total_ref,
+    send, got, ret, slot_row, place_out, place_in, place_row, pick, rows, results,
     proj, up, proj_t, up_t, oacc, dqacc, dk_t, dv_t, low_t, ct_t, dproj, att, terms,
     half_a, own_a, part_a, mine_a, half_b, own_b, part_b, mine_b, sem_a, sem_b, sem,
 ):
@@ -181,7 +182,7 @@
     counts = jnp.dot(hot(owned), hot(before), preferred_element_type=F32)
     earlier = jnp.sum(jnp.where(owned, counts, 0.0), axis=0, keepdims=True)
     slot = owner.astype(F32) * CAP + earlier
-    slot_ref[...] = jnp.broadcast_to(slot, slot_ref.shape)
+    slot_row[...] = jnp.broadcast_to(slot, slot_row.shape)
     high = place // 32
     line = iota((128, ROWS), 0) == earlier
     codes = [
@@ -287,8 +288,8 @@
         hs = chunk(h, 16)
         dk = jnp.zeros((16, ROWS), F32)
         dv = jnp.zeros((16, ROWS), F32)
-        for r in range(NR):
-            rs = slice(r * RC, (r + 1) * RC)
+        for r in range(ROWS // HC):
+            rs = slice(r * HC, (r + 1) * HC)
             qm = proj[g, rs, :] * (mask * BF(0.25))
             um = up[g, rs, :] * mask
             s = dg(qm, k, 1, 1)
@@ -306,17 +307,13 @@
         dk_t[hs, :] = dk.astype(BF)
         dv_t[hs, :] = dv.astype(BF)
 
-        @pl.when(h == 17)
+        @pl.when(h == 16)
         def _():
             sums[0].scatter()
 
-        @pl.when(h == 20)
+        @pl.when(h == 21)
         def _():
             sums[0].gather()
-
-        @pl.when(h == 23)
-        def _():
-            sums[0].give()
 
         @pl.when(h - g * 8 == 7)
         def _():
@@ -347,6 +344,10 @@
     sums[1].pair()
 
     def epilogue(r, _):
+        @pl.when(r == 1)
+        def _():
+            sums[1].scatter()
+
         rs = chunk(r, RC)
         v, n, inv = layer_norm(rows[rs, :C])
         a = jnp.concatenate([att[g, rs, :] for g in range(3)], axis=1)
@@ -360,60 +361,61 @@
         return 0
 
     lax.fori_loop(0, NR, epilogue, 0)
-    sums[1].scatter()
-
-    def send_back(step):
-        tx = lax.rem(sx + step, NX)
-
-        def go(d, _):
-            t = tx * NY + lax.rem(sy + d, NY)
-            copy_to(back.at[chunk(t, CAP)], ret_ref.at[chunk(me, CAP)], t, 6)
-            return 0
-
-        lax.fori_loop(jnp.where(step == 0, 1, 0), NY, go, 0)
-
-    def backs(k, _):
-        tx = lax.rem(sx + k, NX)
-        ss = chunk(tx, SC)
-        spot = jnp.broadcast_to(place_row[0:1, ss], (128, SC)).T[:, 0:1]
-        q = hot(iota((SC, ROWS), 1) == spot)
-        back[ss, :] = jnp.dot(q, results[...], preferred_element_type=F32).astype(BF)
-
-        @pl.when(k > 0)
-        def _():
-            send_back(k - 1)
-
-        return 0
-
-    lax.fori_loop(0, NX // 2, backs, 0)
+    sums[0].give()
     sums[1].gather()
-    lax.fori_loop(NX // 2, NX, backs, 0)
-    send_back(NX - 1)
-    own = pltpu.make_async_copy(back.at[mine], ret_ref.at[mine], sem.at[8])
-    own.start()
-    sums[1].give()
     for part in range(2):
         wait_for(send.at[part, pl.ds(0, SLOTS - CAP)], sem.at[2 * part])
+
+    def backs(part):
+        def step(k, _):
+            tx = lax.rem(sx + k, NX)
+            ss = chunk(tx, SC)
+            spot = jnp.broadcast_to(place_row[0:1, ss], (128, SC)).T[:, 0:1]
+            q = hot(iota((SC, ROWS), 1) == spot)
+            send[part, ss, :] = jnp.dot(
+                q, results[:, part * C : (part + 1) * C], preferred_element_type=F32
+            ).astype(BF)
+
+            @pl.when(k > 0)
+            def _():
+                send_part(part, send, ret, k - 1, 6 + 2 * part)
+
+            return 0
+
+        lax.fori_loop(0, NX, step, 0)
+        send_part(part, send, ret, NX - 1, 6 + 2 * part)
+        ret[part, mine, :] = send[part, mine, :]
+
+    backs(0)
+    backs(1)
+
+    def takes(r, _):
+        rs = chunk(r, RC)
+        spot = jnp.broadcast_to(slot_row[0:1, rs], (128, RC)).T[:, 0:1]
+        pick[rs, :] = hot(iota((RC, SLOTS), 1) == spot)
+        return 0
+
+    lax.fori_loop(0, NR, takes, 0)
+    sums[1].give()
+    for part, dst in enumerate((out_ref, gx_ref)):
+        wait_for(ret.at[part, pl.ds(0, SLOTS - CAP)], sem.at[7 + 2 * part])
+
+        def unpack(r, _, part=part, dst=dst):
+            rs = chunk(r, RC)
+            dst[rs, :] = jnp.dot(pick[rs, :], ret[part], preferred_element_type=F32).astype(BF)
+            return 0
+
+        lax.fori_loop(0, NR, unpack, 0)
     wait_for(place_out.at[pl.ds(0, DEV - 1)], sem.at[4])
-    own.wait()
-    for i in range(6, 8):
-        wait_for(back.at[pl.ds(0, SLOTS - CAP)], sem.at[i])
+    for part in range(2):
+        wait_for(send.at[part, pl.ds(0, SLOTS - CAP)], sem.at[6 + 2 * part])
     sums[0].finish()
     sums[1].finish()
 
 
-def last_kernel(scale, ret_ref, slot_ref, total_ref, out_ref, gx_ref, gq_ref, gp_ref, col):
-    col[...] = jnp.broadcast_to(slot_ref[0:1, :], (128, ROWS)).T
-
-    def step(i, _):
-        rs = chunk(i, RC)
-        q = hot(iota((RC, SLOTS), 1) == col[rs, 0:1])
-        row = jnp.dot(q, ret_ref[...], preferred_element_type=F32).astype(BF)
-        out_ref[rs, :] = row[:, :C]
-        gx_ref[rs, :] = row[:, C:]
-        return 0
-
-    lax.fori_loop(0, NR, step, 0)
+def last_kernel(scale, x_ref, g_ref, total_ref, out_ref, gx_ref, gq_ref, gp_ref):
+    out_ref[...] = x_ref[...]
+    gx_ref[...] = g_ref[...]
     for g in range(3):
         for i in range(4):
             block = total_ref[(4 * g + i) * C : (4 * g + i + 1) * C, :] * scale
@@ -434,20 +436,20 @@
             vm((span[1] // 2, 128), F32), vm((span[2], 128), F32),
         ]
 
-    ret, total, slot = pl.pallas_call(
+    rows_out, rows_grad, total = pl.pallas_call(
         patch_kernel,
-        out_shape=(shape((SLOTS, 2 * C), BF), shape((GROWS, 128), F32), shape((8, ROWS), F32)),
+        out_shape=(shape((ROWS, C), BF), shape((ROWS, C), BF), shape((GROWS, 128), F32)),
         in_specs=[VM] * 5,
-        out_specs=(ANY, ANY, VM),
+        out_specs=(VM, VM, ANY),
         scratch_shapes=[
-            vm((2, SLOTS, C), BF), vm((2, SLOTS, C), BF), vm((SLOTS, 2 * C), BF),
+            vm((2, SLOTS, C), BF), vm((2, SLOTS, C), BF), vm((2, SLOTS, C), BF), vm((8, ROWS), F32),
             vm((DEV, 1, 128), F32), vm((DEV, 1, 128), F32), vm((8, SLOTS), F32),
             vm((ROWS, SLOTS), BF), vm((ROWS, 2 * C), BF), vm((ROWS, 2 * C), BF),
             vm((9, ROWS, 128), BF), vm((3, ROWS, 128), BF), vm((C, ROWS), BF), vm((C, ROWS), BF),
             vm((3, ROWS, 128), F32), vm((3, ROWS, 128), F32), vm((C, ROWS), BF), vm((C, ROWS), BF),
             vm((C, ROWS), BF), vm((C, ROWS), BF), vm((3, 3, ROWS, 128), BF), vm((3, ROWS, 128), BF),
             vm((GROWS, 128), F32),
-        ] + room(FIRST) + room(SECOND) + [dma((9,)), dma((9,)), dma((9,))],
+        ] + room(FIRST) + room(SECOND) + [dma((9,)), dma((9,)), dma((10,))],
         compiler_params=pltpu.CompilerParams(
             vmem_limit_bytes=62 * 1024 * 1024, collective_id=0, has_side_effects=True
         ),
@@ -460,10 +462,9 @@
         ),
         in_specs=[VM] * 3,
         out_specs=(VM,) * 4,
-        scratch_shapes=[vm((ROWS, 128), F32)],
         compiler_params=pltpu.CompilerParams(vmem_limit_bytes=60 * 1024 * 1024),
         name="last",
-    )(ret, slot, total)
+    )(rows_out, rows_grad, total)
 
 
 def solution(mesh):

time: 231 us -> 221 us (0.957)
  Pallas kernels: 230 us -> 220 us
    pallas_call x1, Pallas kernels: 221 us -> 216 us  [on_device(): pl.pallas_call(patch_kernel, out_shape=(shape((ROWS, C), BF), shape((ROWS...]
    pallas_call x1, Pallas kernels: 8.95 us -> 4.36 us  [on_device(): pl.pallas_call(functools.partial(last_kernel, 1.0 / math.sqrt(ROWS * DEV)...]
where the time goes in v3:
time: 221 us
  Pallas kernels  220 us (100%)
    pallas_call x1, Pallas kernels, on_device(): pl.pallas_call(patch_kernel, out_shape=(shape((ROWS, C), BF), shape((ROWS...  216 us

profile of v3, /device:TPU:1, one launch (start us, length us, event | category | flops | bytes accessed | tf_op | source)
XLA Modules:
  0.0 221.0 jit_solution(12794876426230389124)
XLA Ops:
  0.6 216.0 %patch.1 = (bf16[1024,384]{1,0:T(8,128)(2,1)}, bf16[1024,384]{1,0:T(8,128)(2,1)}, f32[5120,128]{1,0:T(8,128)}) custom-call(bf16[1024,384]{1,0:T(8,128)(2,1)} %x_ref.1, bf16[1024,384]{1,0:T(8,128)(2,1)} %ct_ref.1, s32[8,128]{1,0:T(8,128)} %bitcast.1, bf16[384,1152]{1,0:T(8,128)(2,1)} %wqkv_ref.1, bf16[384,384]{1,0:T(8,128)(2,1)} %wproj_ref.1), custom_call_target="tpu_custom_call" | custom-call | tf_op jit(solution)/shard_map/patch/pallas_call | solution.py:439
  216.7 4.4 %last.1 = (bf16[1024,384]{1,0:T(8,128)(2,1)}, bf16[1024,384]{1,0:T(8,128)(2,1)}, f32[384,1152]{1,0:T(8,128)}, f32[384,384]{1,0:T(8,128)}) custom-call(bf16[1024,384]{1,0:T(8,128)(2,1)} %get-tuple-element.7.x_ref, bf16[1024,384]{1,0:T(8,128)(2,1)} %get-tuple-element.8.g_ref, f32[5120,128]{1,0:T(8,128)} %get-tuple-element.9.total_ref), custom_call_target="tpu_custom_call" | custom-call | tf_op jit(solution)/shard_map/last/pallas_call | solution.py:458

commit v4 on v3

--- a/solution.py
+++ b/solution.py
@@ -21,7 +21,7 @@
 CAP = 16
 SLOTS = DEV * CAP
 RC = 256
-HC = 512
+HC = 1024
 NR = ROWS // RC
 SC = NY * CAP
 FIRST = (0, 3072, 24)

time: 221 us -> 218 us (0.986)
  Pallas kernels: 220 us -> 217 us
    pallas_call x1, Pallas kernels: 216 us -> 212 us  [on_device(): pl.pallas_call(patch_kernel, out_shape=(shape((ROWS, C), BF), shape((ROWS...]
where the time goes in v4:
time: 218 us; the launch traced here: 217 us
  Pallas kernels  217 us (100%)
    pallas_call x1, Pallas kernels, on_device(): pl.pallas_call(patch_kernel, out_shape=(shape((ROWS, C), BF), shape((ROWS...  212 us

profile of v4, /device:TPU:1, one launch (start us, length us, event | category | flops | bytes accessed | tf_op | source)
XLA Modules:
  0.0 217.4 jit_solution(14658926968264025548)
XLA Ops:
  0.6 212.4 %patch.1 = (bf16[1024,384]{1,0:T(8,128)(2,1)}, bf16[1024,384]{1,0:T(8,128)(2,1)}, f32[5120,128]{1,0:T(8,128)}) custom-call(bf16[1024,384]{1,0:T(8,128)(2,1)} %x_ref.1, bf16[1024,384]{1,0:T(8,128)(2,1)} %ct_ref.1, s32[8,128]{1,0:T(8,128)} %bitcast.1, bf16[384,1152]{1,0:T(8,128)(2,1)} %wqkv_ref.1, bf16[384,384]{1,0:T(8,128)(2,1)} %wproj_ref.1), custom_call_target="tpu_custom_call" | custom-call | tf_op jit(solution)/shard_map/patch/pallas_call | solution.py:439
  213.1 4.4 %last.1 = (bf16[1024,384]{1,0:T(8,128)(2,1)}, bf16[1024,384]{1,0:T(8,128)(2,1)}, f32[384,1152]{1,0:T(8,128)}, f32[384,384]{1,0:T(8,128)}) custom-call(bf16[1024,384]{1,0:T(8,128)(2,1)} %get-tuple-element.7.x_ref, bf16[1024,384]{1,0:T(8,128)(2,1)} %get-tuple-element.8.g_ref, f32[5120,128]{1,0:T(8,128)} %get-tuple-element.9.total_ref), custom_call_target="tpu_custom_call" | custom-call | tf_op jit(solution)/shard_map/last/pallas_call | solution.py:458

commit v5 on v4

--- a/solution.py
+++ b/solution.py
@@ -362,7 +362,6 @@
 
     lax.fori_loop(0, NR, epilogue, 0)
     sums[0].give()
-    sums[1].gather()
     for part in range(2):
         wait_for(send.at[part, pl.ds(0, SLOTS - CAP)], sem.at[2 * part])
 
@@ -387,6 +386,7 @@
         ret[part, mine, :] = send[part, mine, :]
 
     backs(0)
+    sums[1].gather()
     backs(1)
 
     def takes(r, _):
@@ -396,7 +396,6 @@
         return 0
 
     lax.fori_loop(0, NR, takes, 0)
-    sums[1].give()
     for part, dst in enumerate((out_ref, gx_ref)):
         wait_for(ret.at[part, pl.ds(0, SLOTS - CAP)], sem.at[7 + 2 * part])
 
@@ -406,6 +405,8 @@
             return 0
 
         lax.fori_loop(0, NR, unpack, 0)
+        if part == 0:
+            sums[1].give()
     wait_for(place_out.at[pl.ds(0, DEV - 1)], sem.at[4])
     for part in range(2):
         wait_for(send.at[part, pl.ds(0, SLOTS - CAP)], sem.at[6 + 2 * part])

time: 218 us -> 214 us (0.982)
  Pallas kernels: 217 us -> 213 us
    pallas_call x1, Pallas kernels: 212 us -> 209 us  [on_device(): pl.pallas_call(patch_kernel, out_shape=(shape((ROWS, C), BF), shape((ROWS...]
where the time goes in v5:
time: 214 us
  Pallas kernels  213 us (100%)
    pallas_call x1, Pallas kernels, on_device(): pl.pallas_call(patch_kernel, out_shape=(shape((ROWS, C), BF), shape((ROWS...  209 us
    pallas_call x1, Pallas kernels, on_device(): pl.pallas_call(functools.partial(last_kernel, 1.0 / math.sqrt(ROWS * DEV)...  4.36 us

profile of v5, /device:TPU:1, one launch (start us, length us, event | category | flops | bytes accessed | tf_op | source)
XLA Modules:
  0.0 213.7 jit_solution(7719719606502027841)
XLA Ops:
  0.6 208.7 %patch.1 = (bf16[1024,384]{1,0:T(8,128)(2,1)}, bf16[1024,384]{1,0:T(8,128)(2,1)}, f32[5120,128]{1,0:T(8,128)}) custom-call(bf16[1024,384]{1,0:T(8,128)(2,1)} %x_ref.1, bf16[1024,384]{1,0:T(8,128)(2,1)} %ct_ref.1, s32[8,128]{1,0:T(8,128)} %bitcast.1, bf16[384,1152]{1,0:T(8,128)(2,1)} %wqkv_ref.1, bf16[384,384]{1,0:T(8,128)(2,1)} %wproj_ref.1), custom_call_target="tpu_custom_call" | custom-call | tf_op jit(solution)/shard_map/patch/pallas_call | solution.py:440
  209.4 4.4 %last.1 = (bf16[1024,384]{1,0:T(8,128)(2,1)}, bf16[1024,384]{1,0:T(8,128)(2,1)}, f32[384,1152]{1,0:T(8,128)}, f32[384,384]{1,0:T(8,128)}) custom-call(bf16[1024,384]{1,0:T(8,128)(2,1)} %get-tuple-element.7.x_ref, bf16[1024,384]{1,0:T(8,128)(2,1)} %get-tuple-element.8.g_ref, f32[5120,128]{1,0:T(8,128)} %get-tuple-element.9.total_ref), custom_call_target="tpu_custom_call" | custom-call | tf_op jit(solution)/shard_map/last/pallas_call | solution.py:459
